TPU v7x, 32 devices: a whole 2x2x4 slice. The times are simulated.
32 devices in a mesh: dp: 8 (over z, x), expert: 4 (over y, core).
Axes of the slice: x: 2, y: 2, z: 4, core: 2. Of those that a mesh axis runs over, the one named last changes fastest.
Arguments:
- tokens: bfloat16 [6272, 768], P(('dp', 'expert')), may hold values from -6 to 6
- counts: int32 [32, 2], P(('dp', 'expert')), may hold values from 0 to 4, as said below
- routes: int32 [6272, 2], P(('dp', 'expert')), may hold values from 0 to 31, all different within a row
- priority: int32 [32, 196], P(('dp', 'expert')), may hold values from 0 to 195, each once within a row
- out_grad: bfloat16 [6272, 768], P(('dp', 'expert')), may hold values from -6 to 6
- pre_gain: bfloat16 [768], P(('dp', 'expert')), may hold values from 0.5 to 1.5
- pre_shift: bfloat16 [768], P(('dp', 'expert')), may hold values from -1.5 to 1.5
- w_qkv: bfloat16 [768, 2304], P(('dp', 'expert')), may hold values from -0.21875 to 0.21875
- w_out: bfloat16 [768, 768], P(('dp', 'expert')), may hold values from -0.625 to 0.625
- moe_gain: bfloat16 [768], P(('dp', 'expert')), may hold values from 0.5 to 1.5
- moe_shift: bfloat16 [768], P(('dp', 'expert')), may hold values from -1.5 to 1.5
- w_router: bfloat16 [768, 32], P(('dp', 'expert')), may hold values from -0.15625 to 0.15625
- w_up: bfloat16 [32, 768, 3072], P('expert', 'dp'), may hold values from -0.21875 to 0.21875
- w_down: bfloat16 [32, 3072, 768], P('expert', 'dp'), may hold values from -0.109375 to 0.109375
Outputs:
- out_tokens: bfloat16 [6272, 768], P(('dp', 'expert'))
- d_tokens: float32 [6272, 768], P(('dp', 'expert'))
- d_pre_gain: float32 [768], P(('dp', 'expert'))
- d_pre_shift: float32 [768], P(('dp', 'expert'))
- d_w_qkv: float32 [768, 2304], P(('dp', 'expert'))
- d_w_out: float32 [768, 768], P(('dp', 'expert'))
- d_moe_gain: float32 [768], P(('dp', 'expert'))
- d_moe_shift: float32 [768], P(('dp', 'expert'))
- d_w_router: float32 [768, 32], P(('dp', 'expert'))
- d_w_up: float32 [32, 768, 3072], P('expert', 'dp')
- d_w_down: float32 [32, 3072, 768], P('expert', 'dp')
Inputs may be any that keep to these rules, and one draw needn't show every extreme that they name: counts[s,0] is the number of large images (196 patches) and counts[s,1] of small ones (49 patches) of shard s, laid from the shard's first row, large ones first; counts[s,1] = (196 - 196 counts[s,0]) // 49; counts[s,0] is at most 1. `routes`: the two experts of a row differ. Each row of priority names every rank once; lower ranks take slots first.
All inputs are finite; a program needn't handle non-finite values.
Results may differ from a plain program's by a relative error of at most 0.014.
Values may be sent and summed in bfloat16 or wider, within the bound.
A program may use at most 320 MiB of HBM per device.

v0:
```python
from functools import partial
import math
import jax
import jax.numpy as jnp
from jax import lax
from jax.sharding import PartitionSpec as P

D = 768
HEADS = 12
HEAD_DIM = 64
EXPERTS = 32
PATCH_S = 49
PATCH_L = 196
CAP = 13


def normalize(inputs, scale_vec, shift_vec):
    average = jnp.mean(inputs, axis=-1, keepdims=True)
    centred = inputs - average
    variance = jnp.mean(centred * centred, axis=-1, keepdims=True)
    return centred * lax.rsqrt(variance + 1e-06) * scale_vec + shift_vec


def slot_numbers(chosen, rank_of, usable):
    earlier = (rank_of[:, None] < rank_of[None, :]) & usable[:, None]
    first_ids = chosen[:, 0]
    second_ids = chosen[:, 1]
    slot_first = jnp.sum(
        (earlier & (first_ids[:, None] == first_ids[None, :])).astype(jnp.int32), axis=0
    )
    crossing = usable[:, None] & (first_ids[:, None] == second_ids[None, :])
    slot_second = jnp.sum(
        (earlier & (second_ids[:, None] == second_ids[None, :])).astype(jnp.int32), axis=0
    )
    slot_second = slot_second + jnp.sum(crossing.astype(jnp.int32), axis=0)
    return jnp.stack([slot_first, slot_second], axis=1)


def block_probs(query_blk, seg_blk, key_rows, segment_ids):
    raw_scores = jnp.einsum("qhc,khc->hqk", query_blk, key_rows, preferred_element_type=jnp.float32)
    same_seg = (seg_blk[:, None] == segment_ids[None, :])[None]
    return jax.nn.softmax(
        jnp.where(same_seg, raw_scores * (1.0 / math.sqrt(HEAD_DIM)), -1e30), axis=-1
    )


def body(
    tokens,
    counts,
    routes,
    priority,
    out_grad,
    pre_gain,
    pre_shift,
    w_qkv,
    w_out,
    moe_gain,
    moe_shift,
    w_router,
    w_up,
    w_down,
):
    every = ("dp", "expert")
    dense = lax.all_gather(
        jnp.concatenate(
            [w_qkv, w_out, w_router]
            + [vector[:, None] for vector in (pre_gain, pre_shift, moe_gain, moe_shift)],
            axis=1,
        ),
        every,
        axis=0,
        tiled=True,
    )
    edges = (3 * D, 4 * D, 4 * D + EXPERTS)
    qkv_full, outp_full, router_full = (
        dense[:, : edges[0]],
        dense[:, edges[0] : edges[1]],
        dense[:, edges[1] : edges[2]],
    )
    gain_one, shift_one, gain_two, shift_two = (dense[:, edges[2] + i] for i in range(4))
    up_slice = lax.all_to_all(w_up, "dp", split_axis=2, concat_axis=1, tiled=True)
    row_count = tokens.shape[0]
    scale_factor = 1.0 / math.sqrt(HEAD_DIM)
    positions = jnp.arange(row_count, dtype=jnp.int32)
    large_count = counts[0, 0]
    small_count = counts[0, 1]
    large_end = large_count * PATCH_L
    used_end = large_end + small_count * PATCH_S
    segment_ids = jnp.where(
        positions < large_end,
        positions // PATCH_L,
        jnp.where(positions < used_end, large_count + (positions - large_end) // PATCH_S, -1),
    )
    usable = positions < used_end
    rows_in = tokens.astype(jnp.float32)
    normed_one, pull_one = jax.vjp(
        normalize, rows_in, gain_one.astype(jnp.float32), shift_one.astype(jnp.float32)
    )
    packed_one = normed_one.astype(jnp.bfloat16)
    projected = jnp.dot(packed_one, qkv_full, preferred_element_type=jnp.float32).astype(
        jnp.bfloat16
    )
    queries = projected[:, :D].reshape(row_count, HEADS, HEAD_DIM)
    key_rows = projected[:, D : 2 * D].reshape(row_count, HEADS, HEAD_DIM)
    value_rows = projected[:, 2 * D :].reshape(row_count, HEADS, HEAD_DIM)
    blocks = row_count // PATCH_L
    query_blocks = queries.reshape(blocks, PATCH_L, HEADS, HEAD_DIM)
    seg_blocks = segment_ids.reshape(blocks, PATCH_L)

    def forward_block(operands):
        attn_probs = block_probs(operands[0], operands[1], key_rows, segment_ids)
        return jnp.einsum(
            "hqk,khc->qhc",
            attn_probs.astype(jnp.bfloat16),
            value_rows,
            preferred_element_type=jnp.float32,
        ).astype(jnp.bfloat16)

    mixed_rows = lax.map(forward_block, (query_blocks, seg_blocks)).reshape(row_count, D)
    middle = rows_in + jnp.dot(mixed_rows, outp_full, preferred_element_type=jnp.float32)
    normed_two, pull_two = jax.vjp(
        normalize, middle, gain_two.astype(jnp.float32), shift_two.astype(jnp.float32)
    )
    packed_two = normed_two.astype(jnp.bfloat16)
    router_f32 = router_full.astype(jnp.float32)
    packed_f32 = packed_two.astype(jnp.float32)
    logits = jnp.dot(packed_two, router_full, preferred_element_type=jnp.float32)
    expert_ids = jnp.arange(EXPERTS, dtype=jnp.int32)
    onehot = routes[:, :, None] == expert_ids[None, None, :]
    picked = jnp.sum(jnp.where(onehot, logits[:, None, :], 0.0), axis=2)
    gate_vals = jax.nn.softmax(picked, axis=-1)
    slot_ids = slot_numbers(routes, priority[0], usable)
    kept_mask = usable[:, None] & (slot_ids < CAP)
    slot_total = EXPERTS * CAP
    flat_dest = jnp.where(kept_mask, routes * CAP + slot_ids, slot_total)
    token_of_slot = (
        jnp.full((slot_total + 1,), row_count, jnp.int32)
        .at[flat_dest.reshape(-1)]
        .set(jnp.repeat(positions, 2))
    )
    token_of_slot = token_of_slot[:slot_total]
    padded_rows = jnp.concatenate([packed_two, jnp.zeros((1, D), jnp.bfloat16)], axis=0)
    send_rows = jnp.take(padded_rows, token_of_slot, axis=0).reshape(EXPERTS, CAP, D)
    arrived = lax.all_to_all(send_rows, "expert", split_axis=0, concat_axis=1, tiled=True)
    arrived = lax.all_gather(arrived, "dp", axis=1, tiled=True)
    hidden = jnp.einsum("erd,edf->erf", arrived, up_slice, preferred_element_type=jnp.float32)
    activated, gelu_pull = jax.vjp(partial(jax.nn.gelu, approximate=False), hidden)
    activated = activated.astype(jnp.bfloat16)
    produced = jnp.einsum(
        "erf,efd->erd", activated, w_down, preferred_element_type=jnp.float32
    ).astype(jnp.bfloat16)
    produced = lax.psum_scatter(produced, "dp", scatter_dimension=1, tiled=True)
    returned = lax.all_to_all(produced, "expert", split_axis=1, concat_axis=0, tiled=True)
    flat_back = jnp.concatenate(
        [returned.reshape(slot_total, D), jnp.zeros((1, D), jnp.bfloat16)], axis=0
    )
    first_back = jnp.take(flat_back, flat_dest[:, 0], axis=0).astype(jnp.float32)
    second_back = jnp.take(flat_back, flat_dest[:, 1], axis=0).astype(jnp.float32)
    result = middle + gate_vals[:, 0:1] * first_back + gate_vals[:, 1:2] * second_back
    out_tokens = result.astype(jnp.bfloat16)
    grad_rows = out_grad.astype(jnp.float32)
    gate_grad = jnp.stack(
        [jnp.sum(grad_rows * first_back, axis=1), jnp.sum(grad_rows * second_back, axis=1)], axis=1
    )
    picked_grad = gate_vals * (gate_grad - jnp.sum(gate_vals * gate_grad, axis=1, keepdims=True))
    logit_grad = jnp.sum(jnp.where(onehot, picked_grad[:, :, None], 0.0), axis=1)
    slot_gate = (
        jnp.zeros((slot_total + 1,), jnp.float32)
        .at[flat_dest.reshape(-1)]
        .set(gate_vals.reshape(-1))
    )
    grad_pad = jnp.concatenate([grad_rows, jnp.zeros((1, D), jnp.float32)], axis=0)
    grad_send = (jnp.take(grad_pad, token_of_slot, axis=0) * slot_gate[:slot_total, None]).astype(
        jnp.bfloat16
    )
    grad_arrived = lax.all_to_all(
        grad_send.reshape(EXPERTS, CAP, D), "expert", split_axis=0, concat_axis=1, tiled=True
    )
    grad_arrived = lax.all_gather(grad_arrived, "dp", axis=1, tiled=True)
    down_share = jnp.einsum(
        "erf,erd->efd", activated, grad_arrived, preferred_element_type=jnp.float32
    )
    acted_grad = jnp.einsum(
        "erd,efd->erf", grad_arrived, w_down, preferred_element_type=jnp.float32
    )
    hidden_grad = gelu_pull(acted_grad)[0].astype(jnp.bfloat16)
    up_grad = jnp.einsum("erd,erf->edf", arrived, hidden_grad, preferred_element_type=jnp.float32)
    up_share = lax.all_to_all(
        up_grad.astype(jnp.bfloat16), "dp", split_axis=1, concat_axis=2, tiled=True
    ).astype(jnp.float32)
    input_grad = jnp.einsum(
        "erf,edf->erd", hidden_grad, up_slice, preferred_element_type=jnp.float32
    ).astype(jnp.bfloat16)
    input_grad = lax.psum_scatter(input_grad, "dp", scatter_dimension=1, tiled=True)
    back_grad = lax.all_to_all(input_grad, "expert", split_axis=1, concat_axis=0, tiled=True)
    flat_grad = jnp.concatenate(
        [back_grad.reshape(slot_total, D), jnp.zeros((1, D), jnp.bfloat16)], axis=0
    )
    normed_two_grad = jnp.take(flat_grad, flat_dest[:, 0], axis=0).astype(jnp.float32)
    normed_two_grad = normed_two_grad + jnp.take(flat_grad, flat_dest[:, 1], axis=0).astype(
        jnp.float32
    )
    normed_two_grad = normed_two_grad + jnp.einsum(
        "te,de->td", logit_grad, router_f32, precision=lax.Precision.HIGHEST
    )
    router_grad = jnp.einsum("td,te->de", packed_f32, logit_grad, precision=lax.Precision.HIGHEST)
    middle_part, gain_two_grad, shift_two_grad = pull_two(normed_two_grad)
    middle_grad = grad_rows + middle_part
    branch_grad = middle_grad.astype(jnp.bfloat16)
    out_proj_grad = jnp.einsum(
        "td,te->de", mixed_rows, branch_grad, preferred_element_type=jnp.float32
    )
    mixed_grad = jnp.einsum(
        "te,de->td", branch_grad, outp_full, preferred_element_type=jnp.float32
    ).astype(jnp.bfloat16)
    grad_blocks = mixed_grad.reshape(blocks, PATCH_L, HEADS, HEAD_DIM)

    def backward_block(carried, operands):
        key_acc, value_acc = carried
        query_blk, seg_blk, grad_blk = operands
        attn_probs = block_probs(query_blk, seg_blk, key_rows, segment_ids)
        probs_grad = jnp.einsum(
            "qhc,khc->hqk", grad_blk, value_rows, preferred_element_type=jnp.float32
        )
        value_acc = value_acc + jnp.einsum(
            "hqk,qhc->khc",
            attn_probs.astype(jnp.bfloat16),
            grad_blk,
            preferred_element_type=jnp.float32,
        )
        score_grad = attn_probs * (
            probs_grad - jnp.sum(attn_probs * probs_grad, axis=-1, keepdims=True)
        )
        raw_grad = (score_grad * scale_factor).astype(jnp.bfloat16)
        query_grad = jnp.einsum(
            "hqk,khc->qhc", raw_grad, key_rows, preferred_element_type=jnp.float32
        )
        key_acc = key_acc + jnp.einsum(
            "hqk,qhc->khc", raw_grad, query_blk, preferred_element_type=jnp.float32
        )
        return ((key_acc, value_acc), query_grad)

    zero_heads = jnp.zeros((row_count, HEADS, HEAD_DIM), jnp.float32)
    (key_grad, value_grad), query_grads = lax.scan(
        backward_block, (zero_heads, zero_heads), (query_blocks, seg_blocks, grad_blocks)
    )
    projected_grad = jnp.concatenate(
        [
            query_grads.reshape(row_count, D),
            key_grad.reshape(row_count, D),
            value_grad.reshape(row_count, D),
        ],
        axis=1,
    ).astype(jnp.bfloat16)
    qkv_grad = jnp.einsum(
        "td,te->de", packed_one, projected_grad, preferred_element_type=jnp.float32
    )
    normed_one_grad = jnp.einsum(
        "te,de->td", projected_grad, qkv_full, preferred_element_type=jnp.float32
    )
    rows_part, gain_one_grad, shift_one_grad = pull_one(normed_one_grad)
    tokens_grad = middle_grad + rows_part
    dense_grad = jnp.concatenate(
        [qkv_grad, out_proj_grad, router_grad]
        + [
            vector[:, None]
            for vector in (gain_one_grad, shift_one_grad, gain_two_grad, shift_two_grad)
        ],
        axis=1,
    ).astype(jnp.bfloat16)
    dense_share = lax.psum_scatter(dense_grad, every, scatter_dimension=0, tiled=True).astype(
        jnp.float32
    )
    return (
        out_tokens,
        tokens_grad,
        dense_share[:, edges[2]],
        dense_share[:, edges[2] + 1],
        dense_share[:, : edges[0]],
        dense_share[:, edges[0] : edges[1]],
        dense_share[:, edges[2] + 2],
        dense_share[:, edges[2] + 3],
        dense_share[:, edges[1] : edges[2]],
        up_share,
        down_share,
    )


def solution(mesh):
    placed = (
        P(("dp", "expert"), None),
        P(("dp", "expert"), None),
        P(("dp", "expert"), None),
        P(("dp", "expert"), None),
        P(("dp", "expert"), None),
        P(("dp", "expert")),
        P(("dp", "expert")),
        P(("dp", "expert"), None),
        P(("dp", "expert"), None),
        P(("dp", "expert")),
        P(("dp", "expert")),
        P(("dp", "expert"), None),
        P("expert", "dp", None),
        P("expert", "dp", None),
    )
    return jax.shard_map(
        body,
        mesh=mesh,
        in_specs=placed,
        out_specs=(
            P(("dp", "expert"), None),
            P(("dp", "expert"), None),
            P(("dp", "expert")),
            P(("dp", "expert")),
            P(("dp", "expert"), None),
            P(("dp", "expert"), None),
            P(("dp", "expert")),
            P(("dp", "expert")),
            P(("dp", "expert"), None),
            P("expert", "dp", None),
            P("expert", "dp", None),
        ),
        check_vma=False,
    )
```

profile of v0, /device:TPU:0, one launch (start us, length us, event | category | flops | bytes accessed | tf_op | source)
XLA Modules:
  0.0 902.9 jit_solution(15943545236240041457)
XLA Ops:
  10.2 1.7 concatenate.27
  12.0 1.3 fusion.103
  17.5 2.9 scatter_custom_fusion
  24.0 55.0 %all-gather.4.cloned.1.call-done = bf16[768,3108]{1,0:T(8,128)(2,1)} async-done(((bf16[24,3108]{1,0:T(8,128)(2,1)}), bf16[768,3108]{1,0:T(8,128)(2,1)}) %all-gather.4.cloned.1.call-update) | async-done | bytes 4773904 | tf_op jit(solution)/shard_map/all_gather | solution.py:64
  79.1 2.0 convert_reduce_fusion.2
  81.0 3.1 convolution_convert_fusion.1
  84.8 2.5 fusion.104
  87.3 2.1 convolution_convert_fusion.6
  89.4 1.9 fusion.105
  93.1 2.2 gather_fusion
  95.7 14.2 %all_to_all.93 = bf16[32,13,768]{2,1,0:T(8,128)(2,1)S(1)} all-to-all(bf16[32,13,768]{2,1,0:T(8,128)(2,1)S(1)} %broadcast_select_fusion), channel_id=1, replica_groups=mesh['dp'=8,'expert'=4] {'expert'}, dimensions={0} | all-to-all | bytes 1277952 | tf_op jit(solution)/shard_map/all_to_all | solution.py:144
  111.0 8.6 copy.170
  119.6 198.4 %all_to_all.94 = bf16[8,96,3072]{1,0,2:T(8,128)(2,1)} all-to-all(bf16[8,96,3072]{1,0,2:T(8,128)(2,1)} %copy.170), channel_id=1, replica_groups=mesh['dp'=8,'expert'=4] {'dp'}, dimensions={2} | all-to-all | bytes 9437184 | tf_op jit(solution)/shard_map/all_to_all | solution.py:81
  318.0 8.5 copy.171
  326.5 8.4 fusion.35
  335.0 12.4 %multiply_convert_fusion = (bf16[8,416,384]{2,1,0:T(8,128)(2,1)S(1)}, f32[8,416,384]{2,1,0:T(8,128)}) fusion(f32[8,416,384]{2,1,0:T(8,128)S(1)} %get-tuple-element.109, u8[416,384]{1,0:T(8,128)(4,1)S(1)} %get-tuple-element.54, u8[416,384]{1,0:T(8,128)(4,1)S(1)} %get-tuple-element.53), kind=kLoop, calls=%fused_computation.19 | loop fusion | flops 89456640 | bytes 13099008 | tf_op jit(solution)/shard_map/convert_element_type | solution.py:148
  347.3 5.4 convolution_convert_fusion.3
  352.7 5.2 copy.173
  358.0 100.1 %reduce-scatter.6.cloned.1.call-done = bf16[8,52,768]{2,0,1:T(8,128)(2,1)} async-done(((bf16[8,416,768]{2,0,1:T(8,128)(2,1)}), bf16[8,52,768]{2,0,1:T(8,128)(2,1)}) %reduce-scatter.6.cloned.1.call-update) | async-done | bytes 638992 | tf_op jit(solution)/shard_map/reduce_scatter | solution.py:152
  458.1 4.2 all-to-all-start.2
  463.6 2.5 gather_fusion.1
  466.1 2.5 gather.18
  470.5 1.9 all-to-all-done.2
  472.4 2.1 copy.174
  474.5 2.1 reshape.380
  477.7 1.8 gather_fusion.2
  479.4 1.8 gather_fusion.3
  481.2 1.5 fusion.61
  483.7 3.0 scatter_custom_fusion.1
  486.9 1.6 multiply_convert_fusion.2
  488.5 14.0 %all_to_all.95 = bf16[32,13,768]{2,1,0:T(8,128)(2,1)S(1)} all-to-all(bf16[32,13,768]{2,1,0:T(8,128)(2,1)S(1)} %multiply_convert_fusion.2), channel_id=1, replica_groups=mesh['dp'=8,'expert'=4] {'expert'}, dimensions={0} | all-to-all | bytes 1277952 | tf_op jit(solution)/shard_map/all_to_all | solution.py:176
  503.7 83.1 %all-gather.8.cloned.1.call-done = bf16[8,416,768]{2,0,1:T(8,128)(2,1)} async-done(((bf16[8,52,768]{2,0,1:T(8,128)(2,1)}), bf16[8,416,768]{2,0,1:T(8,128)(2,1)}) %all-gather.8.cloned.1.call-update) | async-done | bytes 5111824 | tf_op jit(solution)/shard_map/all_gather | solution.py:179
  586.7 10.9 %add_convert_fusion = bf16[8,416,384]{2,1,0:T(8,128)(2,1)S(1)} fusion(f32[8,416,384]{2,1,0:T(8,128)} %get-tuple-element.90, f32[8,416,384]{2,1,0:T(8,128)} %copy-done.1, bf16[8,384,768]{2,1,0:T(8,128)(2,1)} %param.29, bf16[8,416,768]{2,0,1:T(8,128)(2,1)} %all-gather.8.cloned.1.call-done), kind=kOutput, calls=%fused_computation.18 | convolution fusion | flops 1980825600 | bytes 22609920 | tf_op jit(solution)/shard_map/erd,efd->erf/dot_general | solution.py:183
  597.6 6.9 convolution_convert_fusion.2
  604.5 5.2 copy.179
  612.4 96.9 %reduce-scatter.8.cloned.1.call-done = bf16[8,52,768]{2,0,1:T(8,128)(2,1)} async-done(((bf16[8,416,768]{2,0,1:T(8,128)(2,1)}), bf16[8,52,768]{2,0,1:T(8,128)(2,1)}) %reduce-scatter.8.cloned.1.call-update) | async-done | bytes 638992 | tf_op jit(solution)/shard_map/reduce_scatter | solution.py:194
  709.3 3.9 all-to-all-start.4
  713.2 6.8 fusion.19
  720.0 5.0 copy.192
  725.0 4.6 all-to-all-start.5
  730.9 2.1 reshape.381
  734.1 1.9 gather_fusion.5
  736.0 1.9 gather_fusion.4
  737.9 2.2 multiply_reduce_fusion.1
  740.8 2.6 fusion.95
  744.2 2.5 convolution_convert_fusion.7
  746.8 1.9 copy.181
  748.7 3.1 fusion.106
  751.8 5.6 fusion.39
  757.4 5.6 fusion.36
  763.0 2.4 convolution_convert_fusion.5
  765.5 3.5 fusion.94
  773.6 1.5 convolution_convert_fusion.4
  775.1 3.1 convolution_convert_fusion
  778.2 8.7 concatenate.33
  787.0 9.3 %fusion.8 = f32[8,384,768]{2,1,0:T(8,128)} fusion(bf16[8,416,384]{2,1,0:T(8,128)(2,1)S(1)} %get-tuple-element.89, bf16[8,416,768]{2,0,1:T(8,128)(2,1)} %all-gather.8.cloned.1.call-done), kind=kOutput, calls=%fused_computation.33 | convolution fusion | flops 1962934272 | bytes 17104896 | tf_op jit(solution)/shard_map/erf,erd->efd/dot_general | solution.py:180
  796.3 43.3 %all-to-all-done.5 = bf16[8,768,384]{2,0,1:T(8,128)(2,1)} async-done(((bf16[8,768,384]{2,0,1:T(8,128)(2,1)}), bf16[8,768,384]{2,0,1:T(8,128)(2,1)}, u32[]{:S(2)}, u32[]{:S(2)}) %all-to-all-start.5) | async-done | bytes 4718624 | tf_op jit(solution)/shard_map/all_to_all | solution.py:188
  839.6 3.0 convert_bitcast_fusion
  842.6 9.1 %copy.193 = f32[8,96,8,384]{3,2,1,0:T(8,128)} copy(f32[8,96,8,384]{3,0,1,2:T(8,128)S(1)} %convert_bitcast_fusion) | data formatting | bytes 18874368 | tf_op jit(solution)/shard_map/convert_element_type | solution.py:190
  851.7 11.0 %reshape.389 = f32[8,96,3072]{2,1,0:T(8,128)} reshape(f32[8,96,8,384]{3,2,1,0:T(8,128)} %copy.193) | data formatting | bytes 18874368 | tf_op jit(solution)/shard_map/convert_element_type | solution.py:190
  863.9 26.0 %reduce-scatter.10.cloned.1.call-done = bf16[24,3108]{1,0:T(8,128)(2,1)} async-done(((bf16[768,3108]{1,0:T(8,128)(2,1)}), bf16[24,3108]{1,0:T(8,128)(2,1)}) %reduce-scatter.10.cloned.1.call-update) | async-done | bytes 149200
  891.5 1.6 slice.141
  893.1 1.4 slice.142
  894.5 1.3 slice.145
  (165 shorter events, 33.8 us)
Async XLA Ops:
  7.2 71.9 %all-gather.4.cloned.1.call-start = ((), (), s32[]{:S(2)}) async-start(), calls=%async_computation.9 | async-start | bytes 5068800 | tf_op jit(solution)/shard_map/all_gather | solution.py:64
  11.9 314.6 %all-gather.6.cloned.1.call-start = ((), (), s32[]{:S(2)}) async-start(), calls=%async_computation.10 | async-start | bytes 5750784 | tf_op jit(solution)/shard_map/all_gather | solution.py:145
  17.5 2.9 copy-start.34
  22.3 61.9 %copy-start.19 = (f32[196]{0:T(256)}, f32[196]{0:T(256)S(1)}, u32[]{:S(2)}) copy-start(f32[196]{0:T(256)S(1)} %broadcast_multiply_fusion.1) | copy-start | bytes 2356
  23.5 0.5 copy-start.27
  23.5 60.7 %copy-start.24 = (f32[196]{0:T(256)}, f32[196]{0:T(256)S(1)}, u32[]{:S(2)}) copy-start(f32[196]{0:T(256)S(1)} %fusion.81) | copy-start | bytes 2356
  81.0 3.6 copy-start.32
  84.4 5.0 copy-start.10
  84.6 4.8 copy-start.15
  84.8 4.6 copy-start.16
  87.3 4.1 copy-start.37
  87.3 2.1 copy-start.2
  89.4 3.7 copy-start.13
  91.4 0.8 copy-start
  91.4 4.3 copy-start.21
  91.6 4.1 copy-start.29
  91.6 4.1 copy-start.26
  92.4 0.7 copy-start.5
  111.0 347.1 %reduce-scatter.6.cloned.1.call-start = ((), (), s32[]{:S(2)}) async-start(), calls=%async_computation.11 | async-start | bytes 5750784 | tf_op jit(solution)/shard_map/reduce_scatter | solution.py:152
  334.9 12.4 %copy-start.1 = (f32[8,416,384]{2,1,0:T(8,128)}, f32[8,416,384]{2,1,0:T(8,128)S(1)}, u32[]{:S(2)}) copy-start(f32[8,416,384]{2,1,0:T(8,128)S(1)} %get-tuple-element.109) | copy-start | bytes 15335428
  357.9 119.7 %copy-start.22 = (s32[1024]{0:T(1024)}, s32[1024]{0:T(1024)S(1)}, u32[]{:S(2)}) copy-start(s32[1024]{0:T(1024)S(1)} %pad_clamp_fusion.1) | copy-start | bytes 12292
  358.0 123.2 %copy-start.30 = (pred[196]{0:T(512)(128)(4,1)}, pred[196]{0:T(512)(128)(4,1)S(1)}, u32[]{:S(2)}) copy-start(pred[196]{0:T(512)(128)(4,1)S(1)} %get-tuple-element.112) | copy-start | bytes 592
  358.0 123.2 %copy-start.31 = (pred[196]{0:T(512)(128)(4,1)}, pred[196]{0:T(512)(128)(4,1)S(1)}, u32[]{:S(2)}) copy-start(pred[196]{0:T(512)(128)(4,1)S(1)} %get-tuple-element.113) | copy-start | bytes 592
  458.1 14.3 %all-to-all-start.2 = ((bf16[8,52,768]{2,0,1:T(8,128)(2,1)}), bf16[8,52,768]{2,0,1:T(8,128)(2,1)}, u32[]{:S(2)}, u32[]{:S(2)}) async-start(bf16[8,52,768]{2,0,1:T(8,128)(2,1)} %reduce-scatter.6.cloned.1.call-done), calls=%async_computation.3 | async-start | bytes 1277952 | tf_op jit(solution)/shard_map/all_to_all | solution.py:153
  462.3 124.5 %all-gather.8.cloned.1.call-start = ((), (), s32[]{:S(2)}) async-start(), calls=%async_computation.12 | async-start | bytes 5750784 | tf_op jit(solution)/shard_map/all_gather | solution.py:179
  462.5 16.9 %copy-start.23 = (s32[1024]{0:T(1024)}, s32[1024]{0:T(1024)S(1)}, u32[]{:S(2)}) copy-start(s32[1024]{0:T(1024)S(1)} %pad_clamp_fusion) | copy-start | bytes 12292
  463.6 6.2 copy-start.17
  503.6 205.7 %reduce-scatter.8.cloned.1.call-start = ((), (), s32[]{:S(2)}) async-start(), calls=%async_computation.13 | async-start | bytes 5750784 | tf_op jit(solution)/shard_map/reduce_scatter | solution.py:194
  597.6 6.9 copy-start.7
  609.7 0.7 copy-start.18
  609.7 1.0 copy-start.6
  709.3 15.7 %all-to-all-start.4 = ((bf16[8,52,768]{2,0,1:T(8,128)(2,1)}), bf16[8,52,768]{2,0,1:T(8,128)(2,1)S(1)}, u32[]{:S(2)}, u32[]{:S(2)}) async-start(bf16[8,52,768]{2,0,1:T(8,128)(2,1)} %reduce-scatter.8.cloned.1.call-done), calls=%async_computation.6 | async-start | bytes 1277952 | tf_op jit(solution)/shard_map/all_to_all | solution.py:195
  725.0 114.6 %all-to-all-start.5 = ((bf16[8,768,384]{2,0,1:T(8,128)(2,1)}), bf16[8,768,384]{2,0,1:T(8,128)(2,1)}, u32[]{:S(2)}, u32[]{:S(2)}) async-start(bf16[8,768,384]{2,0,1:T(8,128)(2,1)} %copy.192), calls=%async_computation.7 | async-start | bytes 9437184 | tf_op jit(solution)/shard_map/all_to_all | solution.py:188
  729.6 160.2 %reduce-scatter.10.cloned.1.call-start = ((), (), s32[]{:S(2)}) async-start(), calls=%async_computation.14 | async-start | bytes 5068800
  737.9 5.5 copy-start.3
  740.1 11.7 %copy-start.38 = (f32[12,196]{1,0:T(8,128)S(1)}, f32[12,196]{1,0:T(8,128)}, u32[]{:S(2)}) copy-start(f32[12,196]{1,0:T(8,128)} %copy-done.37) | copy-start | bytes 28228
  743.5 0.7 copy-start.11
  763.0 2.4 copy-start.20
  763.0 2.4 copy-start.35
  763.0 2.5 copy-start.36
  765.4 3.6 copy-start.28
  765.4 4.4 copy-start.25
  765.5 8.1 copy-start.12
  765.5 8.1 copy-start.14
  765.5 9.6 %copy-start.33 = (f32[768]{0:T(1024)S(1)}, f32[768]{0:T(1024)}, u32[]{:S(2)}) copy-start(f32[768]{0:T(1024)} %copy-done.32) | copy-start | bytes 9220
  769.0 0.8 copy-start.8
  851.7 11.0 %copy-start.4 = (bf16[196,768]{1,0:T(8,128)(2,1)S(1)}, bf16[196,768]{1,0:T(8,128)(2,1)}, u32[]{:S(2)}) copy-start(bf16[196,768]{1,0:T(8,128)(2,1)} %param.20) | copy-start | bytes 903172
  851.7 11.0 %copy-start.9 = (f32[196,768]{1,0:T(8,128)S(1)}, f32[196,768]{1,0:T(8,128)}, u32[]{:S(2)}) copy-start(f32[196,768]{1,0:T(8,128)} %copy-done.8) | copy-start | bytes 1806340
Sparse Core Ops, SparseCore 0:
  12.0 66.9 all-gather.3
  111.1 163.1 all-gather.5
  358.0 100.0 reduce-scatter.5
  503.7 82.9 all-gather.7
  609.9 99.3 reduce-scatter.7
  787.1 102.6 reduce-scatter.9
where the time goes:
time: 912 us; the launch traced here: 903 us
  waiting for transfers between devices  406 us (45%)
  blocking collectives  227 us (25%)
  local copies, waits for them, and re-layouts  119 us (13%)
  matrix products  88.4 us (10%)
  other arithmetic  33.1 us (4%)
  between operations  16.5 us (2%)
  starting transfers between devices  13.3 us (1%)
    all_to_all x1, blocking collectives, body(): lax.all_to_all(w_up, 'dp', split_axis=2, concat_axis=1, tiled=True)  198 us
    reduce_scatter x1, waiting for transfers between devices, body(): produced = lax.psum_scatter(produced, 'dp', scatter_dimension=1, tiled=True)  100 us
    reduce_scatter x1, waiting for transfers between devices, body(): lax.psum_scatter(input_grad, 'dp', scatter_dimension=1, tiled=True)  96.9 us
    all_gather x1, waiting for transfers between devices, body(): grad_arrived = lax.all_gather(grad_arrived, 'dp', axis=1, tiled=True)  83.1 us
    all_gather x1, waiting for transfers between devices, body(): lax.all_gather(jnp.concatenate([w_qkv, w_out, w_router] + [vector[:, None...  55 us
    all_to_all x1, waiting for transfers between devices, body(): lax.all_to_all(up_grad.astype(jnp.bfloat16), 'dp', split_axis=1, concat_a...  43.3 us
    unnamed x7, waiting for transfers between devices  26.1 us
    convert_element_type x2, local copies, waits for them, and re-layouts, body(): up_share = lax.all_to_all(up_grad.astype(jnp.bfloat16), 'dp', split_axis=...  20.1 us
  transfers between devices with their start and end apart: 9, of which 7 were waited for; matrix products, arithmetic and copies ran while one was open for 15% of the time, Pallas kernels for 0%

commit v1 on v0

--- a/solution.py
+++ b/solution.py
@@ -176,7 +176,19 @@
     grad_arrived = lax.all_to_all(
         grad_send.reshape(EXPERTS, CAP, D), "expert", split_axis=0, concat_axis=1, tiled=True
     )
-    grad_arrived = lax.all_gather(grad_arrived, "dp", axis=1, tiled=True)
+    moved, raw_out, current_value = (
+        jax.lax.axis_size("dp"),
+        jax.lax.axis_index("dp"),
+        grad_arrived.shape[1],
+    )
+    w1, side_arr = (grad_arrived, 1)
+    while side_arr < moved:
+        w1 = jnp.concatenate(
+            [w1, jax.lax.ppermute(w1, "dp", [(k, (k - side_arr) % moved) for k in range(moved)])],
+            axis=1,
+        )
+        side_arr = 2 * side_arr
+    grad_arrived = jnp.roll(w1, raw_out * current_value, axis=1)
     down_share = jnp.einsum(
         "erf,erd->efd", activated, grad_arrived, preferred_element_type=jnp.float32
     )

time: 912 us -> 1050 us (1.15)
  waiting for transfers between devices: 406 us -> 478 us
  local copies, waits for them, and re-layouts: 119 us -> 177 us
    ppermute x0 -> x3, waiting for transfers between devices: none -> 150 us  [body(): jax.lax.ppermute(w1, 'dp', [(k, (k - side_arr) % moved) for k in range(mo...]
    all_gather x1 -> x0, waiting for transfers between devices: 83.1 us -> none  [body(): grad_arrived = lax.all_gather(grad_arrived, 'dp', axis=1, tiled=True)]
    concatenate x0 -> x1, local copies, waits for them, and re-layouts: none -> 60.6 us  [body(): grad_arrived = jnp.roll(w1, raw_out * current_value, axis=1)]
    unnamed x7 -> x6, waiting for transfers between devices: 26.1 us -> 23.3 us
  transfers between devices with their start and end apart: 9 -> 11, of which waited for: 7 -> 9; matrix products, arithmetic and copies ran while one was open for 15% -> 13% of each run, Pallas kernels for 0% -> 0%
where the time goes in v1:
time: 1050 us; the launch traced here: 1040 us
  waiting for transfers between devices  478 us (46%)
  blocking collectives  227 us (22%)
  local copies, waits for them, and re-layouts  177 us (17%)
  matrix products  84.8 us (8%)
  other arithmetic  33.9 us (3%)
  starting transfers between devices  19.8 us (2%)
  between operations  16.2 us (2%)
    all_to_all x1, blocking collectives, body(): lax.all_to_all(w_up, 'dp', split_axis=2, concat_axis=1, tiled=True)  198 us
    ppermute x3, waiting for transfers between devices, body(): jax.lax.ppermute(w1, 'dp', [(k, (k - side_arr) % moved) for k in range(mo...  150 us
    reduce_scatter x1, waiting for transfers between devices, body(): lax.psum_scatter(input_grad, 'dp', scatter_dimension=1, tiled=True)  101 us
    reduce_scatter x1, waiting for transfers between devices, body(): produced = lax.psum_scatter(produced, 'dp', scatter_dimension=1, tiled=True)  100 us
    concatenate x1, local copies, waits for them, and re-layouts, body(): grad_arrived = jnp.roll(w1, raw_out * current_value, axis=1)  60.6 us
    all_gather x1, waiting for transfers between devices, body(): lax.all_gather(jnp.concatenate([w_qkv, w_out, w_router] + [vector[:, None...  55 us
    all_to_all x1, waiting for transfers between devices, body(): lax.all_to_all(up_grad.astype(jnp.bfloat16), 'dp', split_axis=1, concat_a...  46.4 us
    unnamed x6, waiting for transfers between devices  23.3 us
  transfers between devices with their start and end apart: 11, of which 9 were waited for; matrix products, arithmetic and copies ran while one was open for 13% of the time, Pallas kernels for 0%

profile of v1, /device:TPU:0, one launch (start us, length us, event | category | flops | bytes accessed | tf_op | source)
XLA Modules:
  0.0 1036.3 jit_solution(12861683037534244128)
XLA Ops:
  10.2 1.7 concatenate.41
  17.5 2.9 scatter_custom_fusion
  24.1 55.0 %all-gather.3.cloned.1.call-done = bf16[768,3108]{1,0:T(8,128)(2,1)} async-done(((bf16[24,3108]{1,0:T(8,128)(2,1)}), bf16[768,3108]{1,0:T(8,128)(2,1)}) %all-gather.3.cloned.1.call-update) | async-done | bytes 4773904 | tf_op jit(solution)/shard_map/all_gather | solution.py:64
  79.1 1.8 convert_reduce_fusion.2
  80.9 3.1 convolution_convert_fusion.1
  84.7 2.4 fusion.106
  87.1 2.1 convolution_convert_fusion.6
  89.3 1.9 fusion.107
  92.3 2.2 gather_fusion
  94.9 14.2 %all_to_all.93 = bf16[32,13,768]{2,1,0:T(8,128)(2,1)S(1)} all-to-all(bf16[32,13,768]{2,1,0:T(8,128)(2,1)S(1)} %broadcast_select_fusion), channel_id=1, replica_groups=mesh['dp'=8,'expert'=4] {'expert'}, dimensions={0} | all-to-all | bytes 1277952 | tf_op jit(solution)/shard_map/all_to_all | solution.py:144
  110.2 8.6 copy.186
  118.8 198.4 %all_to_all.94 = bf16[8,96,3072]{1,0,2:T(8,128)(2,1)} all-to-all(bf16[8,96,3072]{1,0,2:T(8,128)(2,1)} %copy.186), channel_id=1, replica_groups=mesh['dp'=8,'expert'=4] {'dp'}, dimensions={2} | all-to-all | bytes 9437184 | tf_op jit(solution)/shard_map/all_to_all | solution.py:81
  317.2 8.5 copy.187
  325.7 8.5 fusion.35
  334.3 12.4 %multiply_convert_fusion = (bf16[8,416,384]{2,1,0:T(8,128)(2,1)S(1)}, f32[8,416,384]{2,1,0:T(8,128)}) fusion(f32[8,416,384]{2,1,0:T(8,128)S(1)} %get-tuple-element.109, u8[416,384]{1,0:T(8,128)(4,1)S(1)} %get-tuple-element.54, u8[416,384]{1,0:T(8,128)(4,1)S(1)} %get-tuple-element.53), kind=kLoop, calls=%fused_computation.19 | loop fusion | flops 89456640 | bytes 13099008 | tf_op jit(solution)/shard_map/convert_element_type | solution.py:148
  346.7 3.0 convolution_convert_fusion.3
  349.7 5.2 copy.189
  355.0 100.1 %reduce-scatter.6.cloned.1.call-done = bf16[8,52,768]{2,0,1:T(8,128)(2,1)} async-done(((bf16[8,416,768]{2,0,1:T(8,128)(2,1)}), bf16[8,52,768]{2,0,1:T(8,128)(2,1)}) %reduce-scatter.6.cloned.1.call-update) | async-done | bytes 638992 | tf_op jit(solution)/shard_map/reduce_scatter | solution.py:152
  455.1 4.2 all-to-all-start.2
  460.6 2.5 gather_fusion.1
  463.1 2.5 gather.18
  466.9 2.5 all-to-all-done.2
  469.3 2.1 copy.190
  471.5 2.1 reshape.380
  474.7 1.7 gather_fusion.3
  476.4 1.8 gather_fusion.2
  480.0 3.0 scatter_custom_fusion.1
  483.2 1.6 multiply_convert_fusion.2
  484.8 14.0 %all_to_all.95 = bf16[32,13,768]{2,1,0:T(8,128)(2,1)S(1)} all-to-all(bf16[32,13,768]{2,1,0:T(8,128)(2,1)S(1)} %multiply_convert_fusion.2), channel_id=1, replica_groups=mesh['dp'=8,'expert'=4] {'expert'}, dimensions={0} | all-to-all | bytes 1277952 | tf_op jit(solution)/shard_map/all_to_all | solution.py:176
  499.1 3.0 collective-permute-start
  502.2 13.2 %collective-permute-done = bf16[8,52,768]{2,0,1:T(8,128)(2,1)S(1)} collective-permute-done((bf16[8,52,768]{2,0,1:T(8,128)(2,1)S(1)}, bf16[8,52,768]{2,0,1:T(8,128)(2,1)S(1)}, u32[]{:S(2)}, u32[]{:S(2)}) %collective-permute-start) | collective-permute-done | bytes 639008 | tf_op jit(solution)/shard_map/ppermute | solution.py:187
  515.7 1.9 collective-permute-start.1
  517.5 27.0 %collective-permute-done.1 = bf16[8,104,768]{2,1,0:T(8,128)(2,1)S(1)} collective-permute-done((bf16[8,104,768]{2,1,0:T(8,128)(2,1)S(1)}, bf16[8,104,768]{2,1,0:T(8,128)(2,1)S(1)}, u32[]{:S(2)}, u32[]{:S(2)}) %collective-permute-start.1) | collective-permute-done | bytes 1277984 | tf_op jit(solution)/shard_map/ppermute | solution.py:187
  544.6 1.9 pad_maximum_fusion
  548.1 109.5 %collective-permute-done.2 = bf16[8,208,768]{2,1,0:T(8,128)(2,1)} collective-permute-done((bf16[8,208,768]{2,1,0:T(8,128)(2,1)}, bf16[8,208,768]{2,1,0:T(8,128)(2,1)}, u32[]{:S(2)}, u32[]{:S(2)}) %collective-permute-start.2) | collective-permute-done | bytes 2555936 | tf_op jit(solution)/shard_map/ppermute | solution.py:187
  657.6 60.6 %concatenate.47 = bf16[8,832,768]{2,1,0:T(8,128)(2,1)} concatenate(bf16[8,52,768]{2,1,0:T(8,128)(2,1)} %copy-done, bf16[8,52,768]{2,1,0:T(8,128)(2,1)} %copy-done.1, bf16[8,104,768]{2,1,0:T(8,128)(2,1)} %copy-done.2, bf16[8,208,768]{2,1,0:T(8,128)(2,1)} %collective-permute-done.2, bf16[8,52,768]{2,1,0:T(8,128)(2,1)} %copy-done, bf16[8,52,768]{2,1,0:T(8,128)(2,1)} %copy-done.1, ...), dimensions={1} | concatenate | bytes 20447232 | tf_op jit(solution)/shard_map/jit(_roll_dynamic)/concatenate | solution.py:191
  718.2 12.3 %add_convert_fusion = bf16[8,416,384]{2,1,0:T(8,128)(2,1)} fusion(f32[8,416,384]{2,1,0:T(8,128)} %get-tuple-element.90, f32[8,416,384]{2,1,0:T(8,128)} %copy-done.4, bf16[8,384,768]{2,1,0:T(8,128)(2,1)} %param.29, bf16[8,832,768]{2,1,0:T(8,128)(2,1)} %concatenate.47, s32[]{:T(128)S(6)} %select_n.113), kind=kOutput, calls=%fused_computation.18 | convolution fusion | flops 1980825600 | bytes 22609924 | tf_op jit(solution)/shard_map/erd,efd->erf/dot_general | solution.py:195
  730.5 4.6 convolution_convert_fusion.2
  735.1 5.2 copy.202
  742.9 100.8 %reduce-scatter.8.cloned.1.call-done = bf16[8,52,768]{2,0,1:T(8,128)(2,1)} async-done(((bf16[8,416,768]{2,0,1:T(8,128)(2,1)}), bf16[8,52,768]{2,0,1:T(8,128)(2,1)}) %reduce-scatter.8.cloned.1.call-update) | async-done | bytes 638992 | tf_op jit(solution)/shard_map/reduce_scatter | solution.py:206
  843.7 3.9 all-to-all-start.4
  847.6 6.8 fusion.19
  854.4 5.0 copy.215
  859.5 4.6 all-to-all-start.5
  865.3 2.1 reshape.381
  868.6 1.9 gather_fusion.5
  870.4 1.9 gather_fusion.4
  872.3 2.2 multiply_reduce_fusion.1
  875.2 2.6 fusion.97
  879.6 2.5 convolution_convert_fusion.7
  882.2 1.9 copy.204
  884.0 3.1 fusion.108
  887.1 5.6 fusion.36
  892.7 5.6 fusion.39
  898.3 2.4 convolution_convert_fusion.5
  900.8 3.5 fusion.96
  908.8 3.1 convolution_convert_fusion
  911.9 8.7 concatenate.50
  920.6 8.9 fusion.12
  929.5 46.4 %all-to-all-done.5 = bf16[8,768,384]{2,0,1:T(8,128)(2,1)} async-done(((bf16[8,768,384]{2,0,1:T(8,128)(2,1)}), bf16[8,768,384]{2,0,1:T(8,128)(2,1)}, u32[]{:S(2)}, u32[]{:S(2)}) %all-to-all-start.5) | async-done | bytes 4718624 | tf_op jit(solution)/shard_map/all_to_all | solution.py:200
  975.9 3.1 convert_bitcast_fusion
  979.1 9.1 copy.216
  988.2 11.0 %reshape.389 = f32[8,96,3072]{2,1,0:T(8,128)} reshape(f32[8,96,8,384]{3,2,1,0:T(8,128)} %copy.216) | data formatting | bytes 18874368 | tf_op jit(solution)/shard_map/convert_element_type | solution.py:202
  1000.3 23.2 %reduce-scatter.10.cloned.1.call-done = bf16[24,3108]{1,0:T(8,128)(2,1)} async-done(((bf16[768,3108]{1,0:T(8,128)(2,1)}), bf16[24,3108]{1,0:T(8,128)(2,1)}) %reduce-scatter.10.cloned.1.call-update) | async-done | bytes 149200
  (187 shorter events, 40.8 us)
Async XLA Ops:
  7.2 71.9 %all-gather.3.cloned.1.call-start = ((), (), s32[]{:S(2)}) async-start(), calls=%async_computation.9 | async-start | bytes 5068800 | tf_op jit(solution)/shard_map/all_gather | solution.py:64
  11.9 313.8 %all-gather.5.cloned.1.call-start = ((), (), s32[]{:S(2)}) async-start(), calls=%async_computation.10 | async-start | bytes 5750784 | tf_op jit(solution)/shard_map/all_gather | solution.py:145
  17.5 66.6 %copy-start.36 = (s32[392,1]{0,1:T(1,128)}, s32[392,1]{0,1:T(1,128)S(1)}, u32[]{:S(2)}) copy-start(s32[392,1]{0,1:T(1,128)S(1)} %compare_select_fusion.1) | copy-start | bytes 4708
  22.3 61.8 %copy-start.21 = (f32[196]{0:T(256)}, f32[196]{0:T(256)S(1)}, u32[]{:S(2)}) copy-start(f32[196]{0:T(256)S(1)} %broadcast_multiply_fusion.1) | copy-start | bytes 2356
  23.5 0.6 copy-start.29
  23.5 60.6 %copy-start.26 = (f32[196]{0:T(256)}, f32[196]{0:T(256)S(1)}, u32[]{:S(2)}) copy-start(f32[196]{0:T(256)S(1)} %fusion.81) | copy-start | bytes 2356
  80.9 3.4 copy-start.34
  84.3 2.8 copy-start.17
  84.5 4.8 copy-start.18
  84.7 4.6 copy-start.12
  87.1 4.1 copy-start.39
  87.1 2.2 copy-start.5
  89.3 2.3 copy-start.15
  91.2 0.8 copy-start.3
  91.3 3.6 copy-start.23
  91.5 3.4 copy-start.31
  91.5 3.4 copy-start.28
  92.2 16.8 %copy-start.8 = (bf16[196,768]{1,0:T(8,128)(2,1)}, bf16[196,768]{1,0:T(8,128)(2,1)S(1)}, u32[]{:S(2)}) copy-start(bf16[196,768]{1,0:T(8,128)(2,1)S(1)} %add_convert_fusion.1) | copy-start | bytes 903172
  110.1 345.0 %reduce-scatter.6.cloned.1.call-start = ((), (), s32[]{:S(2)}) async-start(), calls=%async_computation.11 | async-start | bytes 5750784 | tf_op jit(solution)/shard_map/reduce_scatter | solution.py:152
  317.2 29.5 %slice-start.2 = ((s8[4718592]{0:T(1024)(128)(4,1)}), s8[524288]{0:T(1024)(128)(4,1)S(1)}, s32[]{:S(2)}) async-start(s8[4718592]{0:T(1024)(128)(4,1)} %bitcast.90), calls=%async_computation.16 | async-start | bytes 1048576
  325.7 21.0 %slice-start.3 = ((s8[4718592]{0:T(1024)(128)(4,1)}), s8[4194304]{0:T(1024)(128)(4,1)S(1)}, s32[]{:S(2)}) async-start(s8[4718592]{0:T(1024)(128)(4,1)} %bitcast.90), calls=%async_computation.17 | async-start | bytes 8388608
  334.3 12.4 %copy-start.4 = (f32[8,416,384]{2,1,0:T(8,128)}, f32[8,416,384]{2,1,0:T(8,128)S(1)}, u32[]{:S(2)}) copy-start(f32[8,416,384]{2,1,0:T(8,128)S(1)} %get-tuple-element.109) | copy-start | bytes 15335428
  354.9 119.7 %copy-start.24 = (s32[1024]{0:T(1024)}, s32[1024]{0:T(1024)S(1)}, u32[]{:S(2)}) copy-start(s32[1024]{0:T(1024)S(1)} %pad_clamp_fusion) | copy-start | bytes 12292
  355.0 123.2 %copy-start.32 = (pred[196]{0:T(512)(128)(4,1)}, pred[196]{0:T(512)(128)(4,1)S(1)}, u32[]{:S(2)}) copy-start(pred[196]{0:T(512)(128)(4,1)S(1)} %get-tuple-element.112) | copy-start | bytes 592
  355.0 123.2 %copy-start.33 = (pred[196]{0:T(512)(128)(4,1)}, pred[196]{0:T(512)(128)(4,1)S(1)}, u32[]{:S(2)}) copy-start(pred[196]{0:T(512)(128)(4,1)S(1)} %get-tuple-element.113) | copy-start | bytes 592
  455.1 14.3 %all-to-all-start.2 = ((bf16[8,52,768]{2,0,1:T(8,128)(2,1)}), bf16[8,52,768]{2,0,1:T(8,128)(2,1)}, u32[]{:S(2)}, u32[]{:S(2)}) async-start(bf16[8,52,768]{2,0,1:T(8,128)(2,1)} %reduce-scatter.6.cloned.1.call-done), calls=%async_computation.3 | async-start | bytes 1277952 | tf_op jit(solution)/shard_map/all_to_all | solution.py:153
  459.2 384.4 %reduce-scatter.8.cloned.1.call-start = ((), (), s32[]{:S(2)}) async-start(), calls=%async_computation.12 | async-start | bytes 5750784 | tf_op jit(solution)/shard_map/reduce_scatter | solution.py:206
  459.5 16.9 %copy-start.25 = (s32[1024]{0:T(1024)}, s32[1024]{0:T(1024)S(1)}, u32[]{:S(2)}) copy-start(s32[1024]{0:T(1024)S(1)} %pad_clamp_fusion.1) | copy-start | bytes 12292
  460.5 6.2 copy-start.19
  499.1 16.3 %collective-permute-start = (bf16[8,52,768]{2,0,1:T(8,128)(2,1)S(1)}, bf16[8,52,768]{2,0,1:T(8,128)(2,1)S(1)}, u32[]{:S(2)}, u32[]{:S(2)}) collective-permute-start(bf16[8,52,768]{2,0,1:T(8,128)(2,1)S(1)} %bitcast.96), channel_id=1, source_target_pairs={{0,28},{4,0},{8,4},{12,8},{16,12},{20,16},{24,20},{28,24},{1,29},{... | collective-permute-start | bytes 1916936 | tf_op jit(solution)/shard_map/ppermute | solution.py:187
  502.2 42.4 %copy-start = (bf16[8,52,768]{2,1,0:T(8,128)(2,1)}, bf16[8,52,768]{2,1,0:T(8,128)(2,1)S(1)}, u32[]{:S(2)}) copy-start(bf16[8,52,768]{2,1,0:T(8,128)(2,1)S(1)} %copy.198) | copy-start | bytes 1916932
  515.5 31.0 %copy-start.1 = (bf16[8,52,768]{2,1,0:T(8,128)(2,1)}, bf16[8,52,768]{2,1,0:T(8,128)(2,1)S(1)}, u32[]{:S(2)}) copy-start(bf16[8,52,768]{2,1,0:T(8,128)(2,1)S(1)} %copy.199) | copy-start | bytes 1916932
  515.7 28.9 %collective-permute-start.1 = (bf16[8,104,768]{2,1,0:T(8,128)(2,1)S(1)}, bf16[8,104,768]{2,1,0:T(8,128)(2,1)S(1)}, u32[]{:S(2)}, u32[]{:S(2)}) collective-permute-start(bf16[8,104,768]{2,1,0:T(8,128)(2,1)S(1)} %pad_maximum_fusion.1), channel_id=1, source_target_pairs={{0,24},{4,28},{8,0},{12,4},{16,8},{20,12},{24,16},{28,20},{1,25},{... | collective-permute-start | bytes 3833864 | tf_op jit(solution)/shard_map/ppermute | solution.py:187
  544.6 3.5 copy-start.2
  546.5 111.1 %collective-permute-start.2 = (bf16[8,208,768]{2,1,0:T(8,128)(2,1)}, bf16[8,208,768]{2,1,0:T(8,128)(2,1)}, u32[]{:S(2)}, u32[]{:S(2)}) collective-permute-start(bf16[8,208,768]{2,1,0:T(8,128)(2,1)} %pad_maximum_fusion), channel_id=1, source_target_pairs={{0,16},{4,20},{8,24},{12,28},{16,0},{20,4},{24,8},{28,12},{1,17},{... | collective-permute-start | bytes 7667720 | tf_op jit(solution)/shard_map/ppermute | solution.py:187
  657.6 72.9 %slice-start = ((s8[4718592]{0:T(1024)(128)(4,1)}), s8[524288]{0:T(1024)(128)(4,1)S(1)}, s32[]{:S(2)}) async-start(s8[4718592]{0:T(1024)(128)(4,1)} %bitcast.87), calls=%async_computation.14 | async-start | bytes 1048576
  718.2 12.3 %slice-start.1 = ((s8[4718592]{0:T(1024)(128)(4,1)}), s8[4194304]{0:T(1024)(128)(4,1)S(1)}, s32[]{:S(2)}) async-start(s8[4718592]{0:T(1024)(128)(4,1)} %bitcast.87), calls=%async_computation.15 | async-start | bytes 8388608
  740.3 0.7 copy-start.20
  740.3 1.0 copy-start.9
  843.7 15.8 %all-to-all-start.4 = ((bf16[8,52,768]{2,0,1:T(8,128)(2,1)}), bf16[8,52,768]{2,0,1:T(8,128)(2,1)S(1)}, u32[]{:S(2)}, u32[]{:S(2)}) async-start(bf16[8,52,768]{2,0,1:T(8,128)(2,1)} %reduce-scatter.8.cloned.1.call-done), calls=%async_computation.6 | async-start | bytes 1277952 | tf_op jit(solution)/shard_map/all_to_all | solution.py:207
  859.5 116.5 %all-to-all-start.5 = ((bf16[8,768,384]{2,0,1:T(8,128)(2,1)}), bf16[8,768,384]{2,0,1:T(8,128)(2,1)}, u32[]{:S(2)}, u32[]{:S(2)}) async-start(bf16[8,768,384]{2,0,1:T(8,128)(2,1)} %copy.215), calls=%async_computation.7 | async-start | bytes 9437184 | tf_op jit(solution)/shard_map/all_to_all | solution.py:200
  864.1 159.5 %reduce-scatter.10.cloned.1.call-start = ((), (), s32[]{:S(2)}) async-start(), calls=%async_computation.13 | async-start | bytes 5068800
  872.3 5.4 copy-start.6
  875.2 11.9 %copy-start.40 = (f32[12,196]{1,0:T(8,128)S(1)}, f32[12,196]{1,0:T(8,128)}, u32[]{:S(2)}) copy-start(f32[12,196]{1,0:T(8,128)} %copy-done.39) | copy-start | bytes 28228
  877.9 1.7 copy-start.13
  898.3 2.4 copy-start.22
  898.3 2.4 copy-start.37
  898.3 2.4 copy-start.38
  900.7 3.6 copy-start.30
  900.7 4.4 copy-start.27
  900.8 6.5 copy-start.14
  900.8 6.5 copy-start.16
  900.8 7.9 copy-start.35
  904.3 0.8 copy-start.10
  988.2 11.0 %copy-start.7 = (bf16[196,768]{1,0:T(8,128)(2,1)S(1)}, bf16[196,768]{1,0:T(8,128)(2,1)}, u32[]{:S(2)}) copy-start(bf16[196,768]{1,0:T(8,128)(2,1)} %param.20) | copy-start | bytes 903172
  988.2 11.0 %copy-start.11 = (f32[196,768]{1,0:T(8,128)S(1)}, f32[196,768]{1,0:T(8,128)}, u32[]{:S(2)}) copy-start(f32[196,768]{1,0:T(8,128)} %copy-done.10) | copy-start | bytes 1806340
Sparse Core Ops, SparseCore 0:
  12.0 66.9 all-gather.2
  110.2 163.1 all-gather.4
  355.0 100.0 reduce-scatter.5
  740.4 103.2 reduce-scatter.7
  920.7 102.7 reduce-scatter.9
